TPU v7x, 128 devices: a whole 4x4x4 slice. The times are simulated.
128 devices in a mesh: cfg: 2 (over z_lo), req: 8 (over z_hi, x), seq: 8 (over y, core).
Axes of the slice: x: 4, y: 4, z: 4 (z_hi: 2, z_lo: 2; z = z_hi * 2 + z_lo), core: 2. Of those that a mesh axis runs over, the one named last changes fastest.
Arguments:
- img_state: bfloat16 [2, 16, 1024, 1536], P('cfg', 'req', 'seq'), may hold values from -6 to 6
- txt_state: bfloat16 [2, 16, 192, 1536], P('cfg', 'req', 'seq'), may hold values from -6 to 6
- cond_vec: float32 [2, 16, 1536], P('cfg'), may hold values from -6 to 6
- text_len: int32 [2, 16], P('cfg', 'req'), may hold values from 38 to 154, as said below
- latent: float32 [16, 1024, 64], P('req', 'seq', 'cfg'), may hold values from -6 to 6
- w_mod: bfloat16 [15360, 1536], P(('req', 'seq')), may hold values from -0.15625 to 0.15625
- w_qkv_img: bfloat16 [3, 1536, 1536], P(None, 'seq')
- w_qkv_txt: bfloat16 [3, 1536, 1536], P(None, 'seq')
- w_attn_out: bfloat16 [1536, 1536], P('seq'), may hold values from -2 to 2
- w_up: bfloat16 [6144, 1536], P(('cfg', 'req', 'seq')), may hold values from -0.15625 to 0.15625
- w_down: bfloat16 [6144, 1536], P(('cfg', 'req', 'seq')), may hold values from -0.078125 to 0.078125
- w_final: bfloat16 [1536, 64], replicated, may hold values from -0.078125 to 0.078125
Outputs:
- velocity: float32 [16, 1024, 64], P('req', 'seq', 'cfg')
- latent_next: float32 [16, 1024, 64], P('req', 'seq', 'cfg')
Inputs may be any that keep to these rules, and one draw needn't show every extreme that they name: Text slot t of prompt p in branch c is live when t < text_len[c, p]; every draw has a length equal to 154.
All inputs are finite; a program needn't handle non-finite values.
Results may differ from a plain program's by a relative error of at most 0.02.
Values may be sent and summed in bfloat16 or wider, within the bound.
No kernel may reach another device: no remote copies, remote signals or barrier semaphores. Data moves between devices by JAX's collectives and lax.ppermute only.
A program may use at most 128 MiB of HBM per device.

v0:
```python
import jax
import jax.numpy as jnp
from jax import lax
from jax.sharding import PartitionSpec as P

HEAD = 64


def partner_2(shard, axis, apart):
    return lax.ppermute(shard, axis, [(i, i ^ 1 << apart) for i in range(lax.axis_size(axis))])


def layer_norm(value):
    mean = jnp.mean(value, axis=-1, keepdims=True)
    centered = value - mean
    spread = jnp.mean(centered * centered, axis=-1, keepdims=True)
    return centered * lax.rsqrt(spread + 1e-06)


def mlp_term(rows_in, up_block, down_block):
    inner = lax.dot_general(
        rows_in, up_block, (((1,), (1,)), ((), ())), preferred_element_type=jnp.float32
    )
    hidden = jax.nn.gelu(inner, approximate=True).astype(jnp.bfloat16)
    return jnp.dot(hidden, down_block, preferred_element_type=jnp.float32)


def local(
    img_state,
    txt_state,
    cond_vec,
    text_len,
    latent,
    w_mod,
    w_qkv_img,
    w_qkv_txt,
    w_attn_out,
    w_up,
    w_down,
    w_final,
):
    prompts_dev = img_state.shape[1]
    img_rows = img_state.shape[2]
    width = img_state.shape[3]
    cond_act = jax.nn.silu(cond_vec[0]).astype(jnp.bfloat16)
    mod_part = lax.dot_general(
        cond_act, w_mod, (((1,), (1,)), ((), ())), preferred_element_type=jnp.float32
    )
    mod_all = lax.all_gather(mod_part, ("req", "seq"), axis=1, tiled=True)
    mine = lax.dynamic_slice_in_dim(mod_all, lax.axis_index("req") * prompts_dev, prompts_dev, 0)
    parts = mine.reshape(prompts_dev, 10, 1, width)
    resid = img_state[0].astype(jnp.float32)
    a_img = (layer_norm(resid) * (1.0 + parts[:, 1]) + parts[:, 0]).astype(jnp.bfloat16)
    a_txt = (
        layer_norm(txt_state[0].astype(jnp.float32)) * (1.0 + parts[:, 7]) + parts[:, 6]
    ).astype(jnp.bfloat16)
    full_img, full_txt = (
        lax.all_gather(a_img, "seq", axis=1, tiled=True),
        lax.all_gather(a_txt, "seq", axis=1, tiled=True),
    )
    proj_img = jnp.einsum(
        "pnd,jed->jpne", full_img, w_qkv_img, preferred_element_type=jnp.float32
    ).astype(jnp.bfloat16)
    proj_txt = jnp.einsum(
        "pnd,jed->jpne", full_txt, w_qkv_txt, preferred_element_type=jnp.float32
    ).astype(jnp.bfloat16)
    total_img = full_img.shape[1]
    local_width = w_qkv_img.shape[1]
    heads_local = local_width // HEAD
    key_heads = jnp.concatenate([proj_img[1], proj_txt[1]], axis=1).reshape(
        prompts_dev, -1, heads_local, HEAD
    )
    value_heads = jnp.concatenate([proj_img[2], proj_txt[2]], axis=1).reshape(
        prompts_dev, -1, heads_local, HEAD
    )
    live = jnp.arange(key_heads.shape[1])[None, :] < (total_img + text_len[0])[:, None]
    block = min(512, total_img)
    queries = proj_img[0].reshape(prompts_dev, total_img // block, block, heads_local, HEAD)

    def attend(query):
        scores = jnp.einsum(
            "pqhe,pkhe->phqk", query, key_heads, preferred_element_type=jnp.float32
        ) * HEAD ** (-0.5)
        scores = jnp.where(live[:, None, None, :], scores, -1e30)
        probs = jax.nn.softmax(scores, axis=-1).astype(jnp.bfloat16)
        return jnp.einsum(
            "phqk,pkhe->pqhe", probs, value_heads, preferred_element_type=jnp.float32
        ).astype(jnp.bfloat16)

    attended = lax.map(attend, jnp.moveaxis(queries, 1, 0))
    attended = jnp.moveaxis(attended, 0, 1).reshape(prompts_dev, total_img, local_width)
    proj = jnp.swapaxes(
        lax.psum_scatter(
            jnp.einsum(
                "pnh,hd->npd", attended, w_attn_out, preferred_element_type=jnp.float32
            ).astype(jnp.bfloat16),
            "seq",
            scatter_dimension=0,
            tiled=True,
        ).astype(jnp.float32),
        0,
        1,
    )
    resid_one = (resid + parts[:, 2] * proj).astype(jnp.bfloat16)
    normed = (layer_norm(resid_one.astype(jnp.float32)) * (1.0 + parts[:, 4]) + parts[:, 3]).astype(
        jnp.bfloat16
    )
    own_rows = normed.reshape(prompts_dev * img_rows, width)
    both = lax.all_gather(own_rows, "cfg", axis=0, tiled=True)
    partial_out = mlp_term(
        both,
        lax.all_gather(w_up, ("req", "seq"), axis=0, tiled=True),
        lax.all_gather(w_down, ("req", "seq"), axis=0, tiled=True),
    )
    mlp_out = lax.psum_scatter(
        partial_out.astype(jnp.bfloat16), "cfg", scatter_dimension=0, tiled=True
    ).astype(jnp.float32)
    mlp_out = mlp_out.reshape(prompts_dev, img_rows, width)
    resid_two = resid_one.astype(jnp.float32) + parts[:, 5] * mlp_out
    final_in = (layer_norm(resid_two) * (1.0 + parts[:, 9]) + parts[:, 8]).astype(jnp.bfloat16)
    branch_vel = jnp.einsum("pnd,dc->pnc", final_in, w_final, preferred_element_type=jnp.float32)
    half_width = latent.shape[2]
    branch_index = lax.axis_index("cfg")
    own_half = lax.dynamic_slice_in_dim(branch_vel, branch_index * half_width, half_width, 2)
    other_half = lax.dynamic_slice_in_dim(
        branch_vel, (1 - branch_index) * half_width, half_width, 2
    )
    partner = partner_2(other_half.astype(jnp.bfloat16), "cfg", 0).astype(other_half.dtype)
    first = branch_index == 0
    cond_vel = jnp.where(first, own_half, partner)
    uncond_vel = jnp.where(first, partner, own_half)
    velocity = uncond_vel + 4.5 * (cond_vel - uncond_vel)
    latent_next = latent - 0.04 * velocity
    return (velocity, latent_next)


def solution(mesh):
    placed = (
        P("cfg", "req", "seq", None),
        P("cfg", "req", "seq", None),
        P("cfg", None, None),
        P("cfg", "req"),
        P("req", "seq", "cfg"),
        P(("req", "seq"), None),
        P(None, "seq", None),
        P(None, "seq", None),
        P("seq", None),
        P(("cfg", "req", "seq"), None),
        P(("cfg", "req", "seq"), None),
        P(),
    )
    return jax.shard_map(
        local,
        mesh=mesh,
        in_specs=placed,
        out_specs=(P("req", "seq", "cfg"), P("req", "seq", "cfg")),
        check_vma=False,
    )
```

profile of v0, /device:TPU:0, one launch (start us, length us, event | category | flops | bytes accessed | tf_op | source)
XLA Modules:
  0.0 504.4 jit_solution(12453538248403719071)
XLA Ops:
  8.0 0.0 copy-start
  8.0 0.0 all-gather.9.cloned.1.call-start
  8.1 1.6 convolution_bitcast_fusion
  9.6 99.6 %all-gather = f32[64,240,16]{1,2,0:T(8,128)S(1)} all-gather(f32[1,240,16]{1,2,0:T(8,128)S(1)} %convolution_bitcast_fusion), channel_id=1, replica_groups=mesh['cfg'=2,'req'=8,'seq'=8] {'req','seq'}, dimensions={0}, use_global_device_ids=true | all-gather | bytes 998400 | tf_op jit(solution)/shard_map/all_gather | solution.py:49
  109.2 1.6 copy.18
  110.8 2.9 reshape.139
  113.7 1.1 dynamic-slice_bitcast_fusion
  114.7 0.1 reshape.131
  114.9 0.7 fusion.119
  115.6 0.1 convert_reduce_fusion.2
  115.7 0.2 fusion.93
  115.9 0.8 fusion.96
  116.7 0.0 all-gather.9.cloned.1.call-update
  116.7 0.0 all-gather.7.cloned.1.call-start
  116.8 0.2 convert_reduce_fusion.1
  117.0 0.3 fusion.75
  117.4 1.3 fusion.78
  118.7 0.0 all-gather.7.cloned.1.call-update
  118.7 0.0 reduce-scatter.3.cloned.1.call-start
  118.8 16.0 %all-gather.9.cloned.1.call-done = bf16[2,192,1536]{2,1,0:T(8,128)(2,1)} async-done(((bf16[2,24,1536]{2,1,0:T(8,128)(2,1)}), bf16[2,192,1536]{2,1,0:T(8,128)(2,1)}) %all-gather.9.cloned.1.call-update) | async-done | bytes 1179664 | tf_op jit(solution)/shard_map/all_gather | solution.py:59
  134.8 2.9 fusion.83
  137.7 0.8 fusion.118
  138.5 39.0 %all-gather.7.cloned.1.call-done = bf16[2,1024,1536]{2,1,0:T(8,128)(2,1)} async-done(((bf16[2,128,1536]{2,1,0:T(8,128)(2,1)}), bf16[2,1024,1536]{2,1,0:T(8,128)(2,1)}) %all-gather.7.cloned.1.call-update) | async-done | bytes 6291472 | tf_op jit(solution)/shard_map/all_gather | solution.py:58
  177.5 6.9 %convert_bitcast_fusion.1 = bf16[3,2,1024,192]{2,3,0,1:T(8,128)(2,1)S(1)} fusion(bf16[2,1024,1536]{2,1,0:T(8,128)(2,1)} %all-gather.7.cloned.1.call-done, bf16[3,192,1536]{2,1,0:T(8,128)(2,1)S(1)} %copy-done), kind=kOutput, calls=%fused_computation.51 | convolution fusion | flops 3625058304 | bytes 10420224 | tf_op jit(solution)/shard_map/pnd,jed->jpne/dot_general | solution.py:61
  184.4 1.4 fusion.117
  185.8 1.5 reshape_squeeze.3
  187.3 2.3 copy.44
  189.6 1.0 pad_maximum_fusion.1
  190.6 1.0 pad_maximum_fusion
  191.6 31.2 %while.11 = (s32[]{:T(128)}, bf16[2,2,512,3,64]{2,4,3,1,0:T(8,128)(2,1)}, bf16[2,2,512,3,64]{2,4,3,1,0:T(8,128)(2,1)}, bf16[2,1216,3,64]{1,3,2,0:T(8,128)(2,1)},...) while((s32[]{:T(128)}, bf16[2,2,512,3,64]{2,4,3,1,0:T(8,128)(2,1)}, ...), condition=%wide.region_7.8_spmd.clone, body=%wide.region_4.7_spmd.clone.sunk | while | flops 1468276480 | bytes 4117205 | solution.py:90
  191.6 0.1 iota_compare_fusion.2
  191.7 7.2 %fusion.142 = f32[2,3,512]{2,1,0:T(4,128)} fusion(pred[2,1216]{1,0:T(4,128)(4,1)S(1)} %iota_compare_fusion.2, bf16[2,1216,3,64]{1,3,2,0:T(8,128)(2,1)} %get-tuple-element.143, bf16[2,2,512,3,64]{2,4,3,1,0:T(8,128)(2,1)} %get-tuple-element.142, s32[]{:T(128)} %get-tuple-element.133), kind=kOutput, calls=%fused_computation.138.clone.1 | convolution fusion | flops 493094080 | bytes 1391488 | tf_op jit(solution)/shard_map/while/body/eval_jaxpr/sub | solution.py:85
  198.9 8.3 %fusion.143 = bf16[2,2,512,3,64]{2,4,3,1,0:T(8,128)(2,1)} fusion(bf16[2,2,512,3,64]{2,4,3,1,0:T(8,128)(2,1)} %get-tuple-element.134, s32[]{:T(128)} %get-tuple-element.133, bf16[2,1216,3,64]{1,3,2,0:T(8,128)(2,1)S(1)} %get-tuple-element.144, f32[2,3,512]{2,1,0:T(4,128)} %fusion.142, pred[2,1216]{1,0:T(4,128)(4,1)S(1)} %iota_compare_fusion.2, ...), kind=kOutput, calls=%fused_computation.13.clone.1 | convolution fusion | flops 975179968 | bytes 2723200 | tf_op jit(solution)/shard_map/while/body/eval_jaxpr/phqk,pkhe->pqhe/dot_general | solution.py:86
  207.2 0.1 iota_compare_fusion.2
  207.3 7.2 %fusion.142 = f32[2,3,512]{2,1,0:T(4,128)} fusion(pred[2,1216]{1,0:T(4,128)(4,1)S(1)} %iota_compare_fusion.2, bf16[2,1216,3,64]{1,3,2,0:T(8,128)(2,1)} %get-tuple-element.143, bf16[2,2,512,3,64]{2,4,3,1,0:T(8,128)(2,1)} %get-tuple-element.142, s32[]{:T(128)} %get-tuple-element.133), kind=kOutput, calls=%fused_computation.138.clone.1 | convolution fusion | flops 493094080 | bytes 1391488 | tf_op jit(solution)/shard_map/while/body/eval_jaxpr/sub | solution.py:85
  214.5 8.3 %fusion.143 = bf16[2,2,512,3,64]{2,4,3,1,0:T(8,128)(2,1)} fusion(bf16[2,2,512,3,64]{2,4,3,1,0:T(8,128)(2,1)} %get-tuple-element.134, s32[]{:T(128)} %get-tuple-element.133, bf16[2,1216,3,64]{1,3,2,0:T(8,128)(2,1)S(1)} %get-tuple-element.144, f32[2,3,512]{2,1,0:T(4,128)} %fusion.142, pred[2,1216]{1,0:T(4,128)(4,1)S(1)} %iota_compare_fusion.2, ...), kind=kOutput, calls=%fused_computation.13.clone.1 | convolution fusion | flops 975179968 | bytes 2723200 | tf_op jit(solution)/shard_map/while/body/eval_jaxpr/phqk,pkhe->pqhe/dot_general | solution.py:86
  222.8 2.8 copy.20
  225.7 2.5 reshape.132
  228.2 5.5 %convert_bitcast_fusion = bf16[1024,2,1536]{2,0,1:T(8,128)(2,1)} fusion(bf16[2,1024,192]{1,2,0:T(8,128)(2,1)S(1)} %reshape.132, bf16[192,1536]{1,0:T(8,128)(2,1)} %param.22), kind=kOutput, calls=%fused_computation.41 | convolution fusion | flops 1211105280 | bytes 7667712 | tf_op jit(solution)/shard_map/pnh,hd->npd/dot_general | solution.py:94
  233.7 0.0 reduce-scatter.3.cloned.1.call-update
  233.7 0.0 all-gather.13.cloned.1.call-start
  233.8 0.5 all-gather.13.cloned.1.call-update
  234.3 0.0 all-gather.15.cloned.1.call-start
  234.4 0.5 all-gather.15.cloned.1.call-update
  234.9 0.0 all-gather.11.cloned.1.call-start
  235.0 43.4 %reduce-scatter.3.cloned.1.call-done = bf16[128,2,1536]{2,0,1:T(8,128)(2,1)} async-done(((bf16[1024,2,1536]{2,0,1:T(8,128)(2,1)}), bf16[128,2,1536]{2,0,1:T(8,128)(2,1)}) %reduce-scatter.3.cloned.1.call-update) | async-done | bytes 786448 | tf_op jit(solution)/shard_map/reduce_scatter | solution.py:93
  278.4 1.5 convert_reduce_fusion
  279.9 0.4 fusion.71
  280.3 1.3 fusion.74
  281.6 0.0 all-gather.11.cloned.1.call-update
  281.6 0.0 copy-start.7
  281.6 0.0 reduce-scatter.5.cloned.1.call-start
  281.7 46.6 %all-gather.13.cloned.1.call-done = bf16[3072,1536]{1,0:T(8,128)(2,1)} async-done(((bf16[48,1536]{1,0:T(8,128)(2,1)}), bf16[3072,1536]{1,0:T(8,128)(2,1)}) %all-gather.13.cloned.1.call-update) | async-done | bytes 9437200 | tf_op jit(solution)/shard_map/all_gather | solution.py:112
  328.3 86.0 %all-gather.15.cloned.1.call-done = bf16[3072,1536]{1,0:T(8,128)(2,1)} async-done(((bf16[48,1536]{1,0:T(8,128)(2,1)}), bf16[3072,1536]{1,0:T(8,128)(2,1)}) %all-gather.15.cloned.1.call-update) | async-done | bytes 9437200 | tf_op jit(solution)/shard_map/all_gather | solution.py:113
  414.3 27.9 %all-gather.11.cloned.1.call-done = bf16[512,1536]{1,0:T(8,128)(2,1)} async-done(((bf16[256,1536]{1,0:T(8,128)(2,1)}), bf16[512,1536]{1,0:T(8,128)(2,1)}) %all-gather.11.cloned.1.call-update) | async-done | bytes 1572880 | tf_op jit(solution)/shard_map/all_gather | solution.py:109
  442.2 18.0 %fusion.57 = bf16[512,1536]{1,0:T(8,128)(2,1)} fusion(bf16[3072,1536]{1,0:T(8,128)(2,1)} %all-gather.15.cloned.1.call-done, bf16[512,1536]{1,0:T(8,128)(2,1)} %all-gather.11.cloned.1.call-done, bf16[3072,1536]{1,0:T(8,128)(2,1)} %all-gather.13.cloned.1.call-done), kind=kOutput, calls=%fused_computation.47 | convolution fusion | flops 9678618624 | bytes 22020096 | tf_op jit(solution)/shard_map/dot_general | solution.py:25
  460.2 0.0 reduce-scatter.5.cloned.1.call-update
  460.3 29.6 %reduce-scatter.5.cloned.1.call-done = bf16[256,1536]{1,0:T(8,128)(2,1)} async-done(((bf16[512,1536]{1,0:T(8,128)(2,1)}), bf16[256,1536]{1,0:T(8,128)(2,1)}) %reduce-scatter.5.cloned.1.call-update) | async-done | bytes 786448 | tf_op jit(solution)/shard_map/reduce_scatter | solution.py:115
  489.9 1.5 fusion.86
  491.5 0.5 multiply_reduce_fusion
  491.9 0.6 fusion.88
  492.6 0.3 collective-permute-start
  492.9 3.5 collective-permute-done
  496.4 0.6 multiply_subtract_fusion
  (47 shorter events, 0.2 us)
Async XLA Ops:
  8.0 169.5 %copy-start = (bf16[3,192,1536]{2,1,0:T(8,128)(2,1)S(1)}, bf16[3,192,1536]{2,1,0:T(8,128)(2,1)}, u32[]{:S(2)}) copy-start(bf16[3,192,1536]{2,1,0:T(8,128)(2,1)} %param.20) | copy-start | bytes 5308420
  8.0 126.8 %all-gather.9.cloned.1.call-start = ((), (), s32[]{:S(2)}) async-start(), calls=%async_computation.3 | async-start | bytes 1327104 | tf_op jit(solution)/shard_map/all_gather | solution.py:59
  110.8 4.8 copy-start.5
  110.8 6.0 %copy-start.1 = (bf16[1,2,128,1536]{3,2,1,0:T(8,128)(2,1)S(1)}, bf16[1,2,128,1536]{3,2,1,0:T(8,128)(2,1)}, u32[]{:S(2)}) copy-start(bf16[1,2,128,1536]{3,2,1,0:T(8,128)(2,1)} %param.14) | copy-start | bytes 2359300
  116.7 60.8 %all-gather.7.cloned.1.call-start = ((), (), s32[]{:S(2)}) async-start(), calls=%async_computation.2 | async-start | bytes 7077888 | tf_op jit(solution)/shard_map/all_gather | solution.py:58
  117.0 1.8 copy-start.15
  118.7 159.7 %reduce-scatter.3.cloned.1.call-start = ((), (), s32[]{:S(2)}) async-start(), calls=%async_computation.4 | async-start | bytes 7077888 | tf_op jit(solution)/shard_map/reduce_scatter | solution.py:93
  187.3 2.3 copy-start.3
  187.3 3.3 copy-start.2
  187.3 3.3 copy-start.6
  233.7 1.2 copy-start.8
  233.7 1.3 copy-start.11
  233.7 1.3 copy-start.12
  233.7 94.6 %all-gather.13.cloned.1.call-start = ((), (), s32[]{:S(2)}) async-start(), calls=%async_computation.6 | async-start | bytes 9584640 | tf_op jit(solution)/shard_map/all_gather | solution.py:112
  234.3 180.0 %all-gather.15.cloned.1.call-start = ((), (), s32[]{:S(2)}) async-start(), calls=%async_computation.7 | async-start | bytes 9584640 | tf_op jit(solution)/shard_map/all_gather | solution.py:113
  234.9 207.3 %all-gather.11.cloned.1.call-start = ((), (), s32[]{:S(2)}) async-start(), calls=%async_computation.5 | async-start | bytes 2359296 | tf_op jit(solution)/shard_map/all_gather | solution.py:109
  281.6 178.7 %copy-start.7 = (f32[2,1,1,1536]{3,1,0,2:T(1,128)S(1)}, f32[2,1,1,1536]{3,1,0,2:T(1,128)}, u32[]{:S(2)}) copy-start(f32[2,1,1,1536]{3,1,0,2:T(1,128)} %get-tuple-element.71) | copy-start | bytes 36868
  281.6 178.7 %copy-start.9 = (f32[2,1,1,1536]{3,1,0,2:T(1,128)S(1)}, f32[2,1,1,1536]{3,1,0,2:T(1,128)}, u32[]{:S(2)}) copy-start(f32[2,1,1,1536]{3,1,0,2:T(1,128)} %get-tuple-element.72) | copy-start | bytes 36868
  281.6 178.7 %copy-start.10 = (f32[2,1,1,1536]{3,1,0,2:T(1,128)S(1)}, f32[2,1,1,1536]{3,1,0,2:T(1,128)}, u32[]{:S(2)}) copy-start(f32[2,1,1,1536]{3,1,0,2:T(1,128)} %get-tuple-element.73) | copy-start | bytes 36868
  281.6 208.3 %reduce-scatter.5.cloned.1.call-start = ((), (), s32[]{:S(2)}) async-start(), calls=%async_computation.8 | async-start | bytes 2359296 | tf_op jit(solution)/shard_map/reduce_scatter | solution.py:115
  460.3 31.7 %copy-start.14 = (bf16[1536,64]{0,1:T(8,128)(2,1)S(1)}, bf16[1536,64]{0,1:T(8,128)(2,1)}, u32[]{:S(2)}) copy-start(bf16[1536,64]{0,1:T(8,128)(2,1)} %param.25) | copy-start | bytes 589828
  489.9 1.6 copy-start.4
  491.9 4.5 copy-start.13
  492.6 3.8 collective-permute-start
Sparse Core Ops, SparseCore 0:
  116.8 17.9 all-gather.8
  136.5 40.9 all-gather.6
  233.8 44.5 reduce-scatter.2
Sparse Core Ops, SparseCore 1:
  237.3 91.0 all-gather.12
  331.3 82.9 all-gather.14
  415.8 26.4 all-gather.10
  460.3 29.5 reduce-scatter.4
where the time goes:
time: 505 us; the launch traced here: 504 us
  waiting for transfers between devices  293 us (58%)
  blocking collectives  99.6 us (20%)
  matrix products  66.5 us (13%)
  local copies, waits for them, and re-layouts  17.2 us (3%)
  between operations  15.8 us (3%)
  other arithmetic  11.6 us (2%)
    all_gather x1, blocking collectives, local(): mod_all = lax.all_gather(mod_part, ('req', 'seq'), axis=1, tiled=True)  99.6 us
    all_gather x1, waiting for transfers between devices, local(): lax.all_gather(w_down, ('req', 'seq'), axis=0, tiled=True)  86 us
    all_gather x1, waiting for transfers between devices, local(): lax.all_gather(w_up, ('req', 'seq'), axis=0, tiled=True)  46.6 us
    reduce_scatter x1, waiting for transfers between devices, local(): lax.psum_scatter(jnp.einsum('pnh,hd->npd', attended, w_attn_out, preferre...  43.4 us
    all_gather x1, waiting for transfers between devices, local(): lax.all_gather(a_img, 'seq', axis=1, tiled=True)  39 us
    reduce_scatter x1, waiting for transfers between devices, local(): lax.psum_scatter(partial_out.astype(jnp.bfloat16), 'cfg', scatter_dimensi...  29.6 us
    all_gather x1, waiting for transfers between devices, local(): both = lax.all_gather(own_rows, 'cfg', axis=0, tiled=True)  27.9 us
    dot_general x1, matrix products, mlp_term(): return jnp.dot(hidden, down_block, preferred_element_type=jnp.float32)  18 us
  transfers between devices with their start and end apart: 8, of which 8 were waited for; matrix products, arithmetic and copies ran while one was open for 2% of the time, Pallas kernels for 0%

commit v1 on v0

--- a/solution.py
+++ b/solution.py
@@ -4,6 +4,27 @@
 from jax.sharding import PartitionSpec as P
 
 HEAD = 64
+
+
+def ring_gather(array, axis, dim):
+    size, here, rows = (lax.axis_size(axis), lax.axis_index(axis), array.shape[dim])
+    right = [(i, (i + 1) % size) for i in range(size)]
+    left = [(i, (i - 1) % size) for i in range(size)]
+    filled = jnp.zeros((*array.shape[:dim], size * rows, *array.shape[dim + 1 :]), array.dtype)
+    filled = lax.dynamic_update_slice_in_dim(filled, array, here * rows, axis=dim)
+    from_left = from_right = array
+    half = size // 2
+    for turn in range(1, half + 1):
+        from_left = lax.ppermute(from_left, axis, right)
+        filled = lax.dynamic_update_slice_in_dim(
+            filled, from_left, (here - turn) % size * rows, axis=dim
+        )
+        if turn < size - half:
+            from_right = lax.ppermute(from_right, axis, left)
+            filled = lax.dynamic_update_slice_in_dim(
+                filled, from_right, (here + turn) % size * rows, axis=dim
+            )
+    return filled
 
 
 def partner_2(shard, axis, apart):
@@ -56,7 +77,7 @@
     ).astype(jnp.bfloat16)
     full_img, full_txt = (
         lax.all_gather(a_img, "seq", axis=1, tiled=True),
-        lax.all_gather(a_txt, "seq", axis=1, tiled=True),
+        ring_gather(a_txt, "seq", 1),
     )
     proj_img = jnp.einsum(
         "pnd,jed->jpne", full_img, w_qkv_img, preferred_element_type=jnp.float32

time: 505 us -> 482 us (0.954)
  waiting for transfers between devices: 293 us -> 255 us
  starting transfers between devices: 0.63 us -> 10.6 us
  local copies, waits for them, and re-layouts: 17.2 us -> 23.3 us
    all_gather x1, waiting for transfers between devices: 39 us -> 2.06 us  [local(): lax.all_gather(a_img, 'seq', axis=1, tiled=True)]
    ppermute x0 -> x7, waiting for transfers between devices: none -> 18.4 us  [the longest x4 9.65 us: ring_gather(): from_left = lax.ppermute(from_left, axis, right)]
    all_gather x1 -> x0, waiting for transfers between devices: 16 us -> none  [local(): lax.all_gather(a_txt, 'seq', axis=1, tiled=True)]
    ppermute x0 -> x7, starting transfers between devices: none -> 10 us  [the longest x3 9.64 us: ring_gather(): from_right = lax.ppermute(from_right, axis, left)]
  transfers between devices with their start and end apart: 8 -> 14, of which waited for: 8 -> 14; matrix products, arithmetic and copies ran while one was open for 2% -> 2% of each run, Pallas kernels for 0% -> 0%
where the time goes in v1:
time: 482 us; the launch traced here: 481 us
  waiting for transfers between devices  255 us (53%)
  blocking collectives  99.6 us (21%)
  matrix products  66 us (14%)
  local copies, waits for them, and re-layouts  23.3 us (5%)
  between operations  15.9 us (3%)
  other arithmetic  11 us (2%)
  starting transfers between devices  10.6 us (2%)
    all_gather x1, blocking collectives, local(): mod_all = lax.all_gather(mod_part, ('req', 'seq'), axis=1, tiled=True)  99.6 us
    all_gather x1, waiting for transfers between devices, local(): lax.all_gather(w_down, ('req', 'seq'), axis=0, tiled=True)  86 us
    all_gather x1, waiting for transfers between devices, local(): lax.all_gather(w_up, ('req', 'seq'), axis=0, tiled=True)  46.7 us
    reduce_scatter x1, waiting for transfers between devices, local(): lax.psum_scatter(jnp.einsum('pnh,hd->npd', attended, w_attn_out, preferre...  40.3 us
    reduce_scatter x1, waiting for transfers between devices, local(): lax.psum_scatter(partial_out.astype(jnp.bfloat16), 'cfg', scatter_dimensi...  28.9 us
    all_gather x1, waiting for transfers between devices, local(): both = lax.all_gather(own_rows, 'cfg', axis=0, tiled=True)  27.9 us
    dot_general x1, matrix products, mlp_term(): return jnp.dot(hidden, down_block, preferred_element_type=jnp.float32)  18 us
    dot_general x2, matrix products, attend(): jnp.einsum('phqk,pkhe->pqhe', probs, value_heads, preferred_element_type=...  16.6 us
  transfers between devices with their start and end apart: 14, of which 14 were waited for; matrix products, arithmetic and copies ran while one was open for 2% of the time, Pallas kernels for 0%

profile of v1, /device:TPU:0, one launch (start us, length us, event | category | flops | bytes accessed | tf_op | source)
XLA Modules:
  0.0 481.3 jit_solution(11907795216637875949)
XLA Ops:
  8.1 1.6 convolution_bitcast_fusion
  9.6 99.6 %all-gather = f32[64,240,16]{1,2,0:T(8,128)S(1)} all-gather(f32[1,240,16]{1,2,0:T(8,128)S(1)} %convolution_bitcast_fusion), channel_id=1, replica_groups=mesh['cfg'=2,'req'=8,'seq'=8] {'req','seq'}, dimensions={0}, use_global_device_ids=true | all-gather | bytes 998400 | tf_op jit(solution)/shard_map/all_gather | solution.py:70
  109.2 1.6 copy.18
  110.8 1.9 reshape.139
  112.7 0.7 dynamic-slice_bitcast_fusion
  113.4 1.0 reshape.131
  114.4 0.7 fusion.120
  115.3 0.3 fusion.75
  115.7 1.3 fusion.78
  117.2 0.2 fusion.93
  117.7 1.0 copy-done.6
  118.7 0.3 collective-permute-start
  119.1 2.6 collective-permute-start.1
  121.7 2.8 collective-permute-done
  124.5 2.8 collective-permute-done.1
  127.2 3.5 collective-permute-start.3
  130.8 0.7 constant_dynamic-update-slice_fusion.6
  131.5 0.7 constant_dynamic-update-slice_fusion.5
  132.1 1.3 collective-permute-done.2
  133.4 3.2 collective-permute-done.3
  136.6 3.5 collective-permute-start.5
  140.1 0.7 constant_dynamic-update-slice_fusion.4
  140.7 0.7 constant_dynamic-update-slice_fusion.3
  141.4 0.9 collective-permute-done.4
  142.3 0.7 constant_dynamic-update-slice_fusion.2
  143.0 2.9 collective-permute-done.5
  145.9 0.7 constant_dynamic-update-slice_fusion.1
  146.5 4.7 collective-permute-done.6
  151.2 0.7 constant_dynamic-update-slice_fusion
  151.9 2.4 fusion.83
  154.3 0.8 fusion.119
  155.1 2.1 all-gather.6.cloned.1.call-done
  157.2 6.8 %convert_bitcast_fusion.1 = bf16[3,2,1024,192]{2,3,0,1:T(8,128)(2,1)S(1)} fusion(bf16[2,1024,1536]{2,1,0:T(8,128)(2,1)} %all-gather.6.cloned.1.call-done, bf16[3,192,1536]{2,1,0:T(8,128)(2,1)S(1)} %copy-done), kind=kOutput, calls=%fused_computation.51 | convolution fusion | flops 3625058304 | bytes 10420224 | tf_op jit(solution)/shard_map/pnd,jed->jpne/dot_general | solution.py:82
  164.0 1.5 fusion.118
  165.5 1.5 reshape_squeeze.3
  167.0 2.3 copy.44
  169.3 1.0 pad_maximum_fusion.1
  170.3 1.0 pad_maximum_fusion
  171.3 31.2 %while.11 = (s32[]{:T(128)}, bf16[2,2,512,3,64]{2,4,3,1,0:T(8,128)(2,1)}, bf16[2,2,512,3,64]{2,4,3,1,0:T(8,128)(2,1)}, bf16[2,1216,3,64]{1,3,2,0:T(8,128)(2,1)},...) while((s32[]{:T(128)}, bf16[2,2,512,3,64]{2,4,3,1,0:T(8,128)(2,1)}, ...), condition=%wide.region_7.8_spmd.clone, body=%wide.region_4.7_spmd.clone.sunk | while | flops 1468276480 | bytes 4117205 | solution.py:111
  171.4 7.2 %fusion.143 = f32[2,3,512]{2,1,0:T(4,128)} fusion(pred[2,1216]{1,0:T(4,128)(4,1)S(1)} %iota_compare_fusion.2, bf16[2,1216,3,64]{1,3,2,0:T(8,128)(2,1)} %get-tuple-element.145, bf16[2,2,512,3,64]{2,4,3,1,0:T(8,128)(2,1)} %get-tuple-element.144, s32[]{:T(128)} %get-tuple-element.135), kind=kOutput, calls=%fused_computation.146.clone.1 | convolution fusion | flops 493094080 | bytes 1391488 | tf_op jit(solution)/shard_map/while/body/eval_jaxpr/sub | solution.py:106
  178.6 8.3 %fusion.144 = bf16[2,2,512,3,64]{2,4,3,1,0:T(8,128)(2,1)} fusion(bf16[2,2,512,3,64]{2,4,3,1,0:T(8,128)(2,1)} %get-tuple-element.136, s32[]{:T(128)} %get-tuple-element.135, bf16[2,1216,3,64]{1,3,2,0:T(8,128)(2,1)S(1)} %get-tuple-element.146, f32[2,3,512]{2,1,0:T(4,128)} %fusion.143, pred[2,1216]{1,0:T(4,128)(4,1)S(1)} %iota_compare_fusion.2, ...), kind=kOutput, calls=%fused_computation.13.clone.1 | convolution fusion | flops 975179968 | bytes 2723200 | tf_op jit(solution)/shard_map/while/body/eval_jaxpr/phqk,pkhe->pqhe/dot_general | solution.py:107
  187.0 7.2 %fusion.143 = f32[2,3,512]{2,1,0:T(4,128)} fusion(pred[2,1216]{1,0:T(4,128)(4,1)S(1)} %iota_compare_fusion.2, bf16[2,1216,3,64]{1,3,2,0:T(8,128)(2,1)} %get-tuple-element.145, bf16[2,2,512,3,64]{2,4,3,1,0:T(8,128)(2,1)} %get-tuple-element.144, s32[]{:T(128)} %get-tuple-element.135), kind=kOutput, calls=%fused_computation.146.clone.1 | convolution fusion | flops 493094080 | bytes 1391488 | tf_op jit(solution)/shard_map/while/body/eval_jaxpr/sub | solution.py:106
  194.2 8.3 %fusion.144 = bf16[2,2,512,3,64]{2,4,3,1,0:T(8,128)(2,1)} fusion(bf16[2,2,512,3,64]{2,4,3,1,0:T(8,128)(2,1)} %get-tuple-element.136, s32[]{:T(128)} %get-tuple-element.135, bf16[2,1216,3,64]{1,3,2,0:T(8,128)(2,1)S(1)} %get-tuple-element.146, f32[2,3,512]{2,1,0:T(4,128)} %fusion.143, pred[2,1216]{1,0:T(4,128)(4,1)S(1)} %iota_compare_fusion.2, ...), kind=kOutput, calls=%fused_computation.13.clone.1 | convolution fusion | flops 975179968 | bytes 2723200 | tf_op jit(solution)/shard_map/while/body/eval_jaxpr/phqk,pkhe->pqhe/dot_general | solution.py:107
  202.5 2.8 copy.20
  205.4 2.5 reshape.132
  207.9 5.5 %convert_bitcast_fusion = bf16[1024,2,1536]{2,0,1:T(8,128)(2,1)} fusion(bf16[2,1024,192]{1,2,0:T(8,128)(2,1)S(1)} %reshape.132, bf16[192,1536]{1,0:T(8,128)(2,1)} %param.22), kind=kOutput, calls=%fused_computation.41 | convolution fusion | flops 1211105280 | bytes 7667712 | tf_op jit(solution)/shard_map/pnh,hd->npd/dot_general | solution.py:115
  213.5 0.5 all-gather.10.cloned.1.call-update
  214.1 0.5 all-gather.12.cloned.1.call-update
  214.8 40.3 %reduce-scatter.3.cloned.1.call-done = bf16[128,2,1536]{2,0,1:T(8,128)(2,1)} async-done(((bf16[1024,2,1536]{2,0,1:T(8,128)(2,1)}), bf16[128,2,1536]{2,0,1:T(8,128)(2,1)}) %reduce-scatter.3.cloned.1.call-update) | async-done | bytes 786448 | tf_op jit(solution)/shard_map/reduce_scatter | solution.py:114
  255.1 1.5 convert_reduce_fusion
  256.6 0.4 fusion.71
  256.9 1.3 fusion.74
  258.3 46.7 %all-gather.10.cloned.1.call-done = bf16[3072,1536]{1,0:T(8,128)(2,1)} async-done(((bf16[48,1536]{1,0:T(8,128)(2,1)}), bf16[3072,1536]{1,0:T(8,128)(2,1)}) %all-gather.10.cloned.1.call-update) | async-done | bytes 9437200 | tf_op jit(solution)/shard_map/all_gather | solution.py:133
  305.0 86.0 %all-gather.12.cloned.1.call-done = bf16[3072,1536]{1,0:T(8,128)(2,1)} async-done(((bf16[48,1536]{1,0:T(8,128)(2,1)}), bf16[3072,1536]{1,0:T(8,128)(2,1)}) %all-gather.12.cloned.1.call-update) | async-done | bytes 9437200 | tf_op jit(solution)/shard_map/all_gather | solution.py:134
  390.9 27.9 %all-gather.8.cloned.1.call-done = bf16[512,1536]{1,0:T(8,128)(2,1)} async-done(((bf16[256,1536]{1,0:T(8,128)(2,1)}), bf16[512,1536]{1,0:T(8,128)(2,1)}) %all-gather.8.cloned.1.call-update) | async-done | bytes 1572880 | tf_op jit(solution)/shard_map/all_gather | solution.py:130
  418.9 18.0 %fusion.57 = bf16[512,1536]{1,0:T(8,128)(2,1)} fusion(bf16[3072,1536]{1,0:T(8,128)(2,1)} %all-gather.12.cloned.1.call-done, bf16[512,1536]{1,0:T(8,128)(2,1)} %all-gather.8.cloned.1.call-done, bf16[3072,1536]{1,0:T(8,128)(2,1)} %all-gather.10.cloned.1.call-done), kind=kOutput, calls=%fused_computation.47 | convolution fusion | flops 9678618624 | bytes 22020096 | tf_op jit(solution)/shard_map/dot_general | solution.py:46
  436.9 0.7 copy-done.8
  437.6 28.9 %reduce-scatter.5.cloned.1.call-done = bf16[256,1536]{1,0:T(8,128)(2,1)} async-done(((bf16[512,1536]{1,0:T(8,128)(2,1)}), bf16[256,1536]{1,0:T(8,128)(2,1)}) %reduce-scatter.5.cloned.1.call-update) | async-done | bytes 786448 | tf_op jit(solution)/shard_map/reduce_scatter | solution.py:136
  466.5 1.6 fusion.86
  468.1 0.5 multiply_reduce_fusion
  468.6 0.6 fusion.88
  469.2 0.3 collective-permute-start.7
  469.6 3.5 collective-permute-done.7
  473.0 0.6 multiply_subtract_fusion
  (70 shorter events, 1.2 us)
Async XLA Ops:
  8.0 149.2 %copy-start = (bf16[3,192,1536]{2,1,0:T(8,128)(2,1)S(1)}, bf16[3,192,1536]{2,1,0:T(8,128)(2,1)}, u32[]{:S(2)}) copy-start(bf16[3,192,1536]{2,1,0:T(8,128)(2,1)} %param.20) | copy-start | bytes 5308420
  8.0 149.2 %all-gather.6.cloned.1.call-start = ((), (), s32[]{:S(2)}) async-start(), calls=%async_computation.2 | async-start | bytes 7077888 | tf_op jit(solution)/shard_map/all_gather | solution.py:79
  110.8 4.3 copy-start.1
  115.3 1.8 copy-start.5
  117.0 4.6 copy-start.17
  117.0 138.0 %reduce-scatter.3.cloned.1.call-start = ((), (), s32[]{:S(2)}) async-start(), calls=%async_computation.3 | async-start | bytes 7077888 | tf_op jit(solution)/shard_map/reduce_scatter | solution.py:114
  117.7 1.0 copy-start.6
  118.7 5.8 %collective-permute-start = (bf16[2,24,1536]{2,1,0:T(8,128)(2,1)S(1)}, bf16[2,24,1536]{2,1,0:T(8,128)(2,1)S(1)}, u32[]{:S(2)}, u32[]{:S(2)}) collective-permute-start(bf16[2,24,1536]{2,1,0:T(8,128)(2,1)S(1)} %get-tuple-element.67), channel_id=1, source_target_pairs={{0,1},{1,2},{2,3},{3,4},{4,5},{5,6},{6,7},{7,0},{8,9},{9,10},{10,1... | collective-permute-start | bytes 442376 | tf_op jit(solution)/shard_map/ppermute | solution.py:18
  119.1 8.2 %collective-permute-start.1 = (bf16[2,24,1536]{2,1,0:T(8,128)(2,1)S(1)}, bf16[2,24,1536]{2,1,0:T(8,128)(2,1)S(1)}, u32[]{:S(2)}, u32[]{:S(2)}) collective-permute-start(bf16[2,24,1536]{2,1,0:T(8,128)(2,1)S(1)} %get-tuple-element.67), channel_id=1, source_target_pairs={{0,7},{1,0},{2,1},{3,2},{4,3},{5,4},{6,5},{7,6},{8,15},{9,8},{10,9... | collective-permute-start | bytes 442376 | tf_op jit(solution)/shard_map/ppermute | solution.py:23
  121.7 30.2 %copy-start.15 = (bf16[3,192,1536]{2,1,0:T(8,128)(2,1)S(1)}, bf16[3,192,1536]{2,1,0:T(8,128)(2,1)}, u32[]{:S(2)}) copy-start(bf16[3,192,1536]{2,1,0:T(8,128)(2,1)} %param.21) | copy-start | bytes 5308420
  124.5 8.9 %collective-permute-start.2 = (bf16[2,24,1536]{2,1,0:T(8,128)(2,1)S(1)}, bf16[2,24,1536]{2,1,0:T(8,128)(2,1)S(1)}, u32[]{:S(2)}, u32[]{:S(2)}) collective-permute-start(bf16[2,24,1536]{2,1,0:T(8,128)(2,1)S(1)} %collective-permute-done), channel_id=1, source_target_pairs={{0,1},{1,2},{2,3},{3,4},{4,5},{5,6},{6,7},{7,0},{8,9},{9,10},{10,1... | collective-permute-start | bytes 442376 | tf_op jit(solution)/shard_map/ppermute | solution.py:18
  127.2 9.3 %collective-permute-start.3 = (bf16[2,24,1536]{2,1,0:T(8,128)(2,1)S(1)}, bf16[2,24,1536]{2,1,0:T(8,128)(2,1)S(1)}, u32[]{:S(2)}, u32[]{:S(2)}) collective-permute-start(bf16[2,24,1536]{2,1,0:T(8,128)(2,1)S(1)} %collective-permute-done.1), channel_id=1, source_target_pairs={{0,7},{1,0},{2,1},{3,2},{4,3},{5,4},{6,5},{7,6},{8,15},{9,8},{10,9... | collective-permute-start | bytes 442376 | tf_op jit(solution)/shard_map/ppermute | solution.py:23
  133.4 8.9 %collective-permute-start.4 = (bf16[2,24,1536]{2,1,0:T(8,128)(2,1)S(1)}, bf16[2,24,1536]{2,1,0:T(8,128)(2,1)S(1)}, u32[]{:S(2)}, u32[]{:S(2)}) collective-permute-start(bf16[2,24,1536]{2,1,0:T(8,128)(2,1)S(1)} %collective-permute-done.2), channel_id=1, source_target_pairs={{0,1},{1,2},{2,3},{3,4},{4,5},{5,6},{6,7},{7,0},{8,9},{9,10},{10,1... | collective-permute-start | bytes 442376 | tf_op jit(solution)/shard_map/ppermute | solution.py:18
  136.6 9.3 %collective-permute-start.5 = (bf16[2,24,1536]{2,1,0:T(8,128)(2,1)S(1)}, bf16[2,24,1536]{2,1,0:T(8,128)(2,1)S(1)}, u32[]{:S(2)}, u32[]{:S(2)}) collective-permute-start(bf16[2,24,1536]{2,1,0:T(8,128)(2,1)S(1)} %collective-permute-done.3), channel_id=1, source_target_pairs={{0,7},{1,0},{2,1},{3,2},{4,3},{5,4},{6,5},{7,6},{8,15},{9,8},{10,9... | collective-permute-start | bytes 442376 | tf_op jit(solution)/shard_map/ppermute | solution.py:23
  142.3 8.9 %collective-permute-start.6 = (bf16[2,24,1536]{2,1,0:T(8,128)(2,1)S(1)}, bf16[2,24,1536]{2,1,0:T(8,128)(2,1)S(1)}, u32[]{:S(2)}, u32[]{:S(2)}) collective-permute-start(bf16[2,24,1536]{2,1,0:T(8,128)(2,1)S(1)} %collective-permute-done.4), channel_id=1, source_target_pairs={{0,1},{1,2},{2,3},{3,4},{4,5},{5,6},{6,7},{7,0},{8,9},{9,10},{10,1... | collective-permute-start | bytes 442376 | tf_op jit(solution)/shard_map/ppermute | solution.py:18
  167.0 2.3 copy-start.3
  167.0 3.3 copy-start.2
  167.0 3.3 copy-start.7
  213.4 1.2 copy-start.9
  213.4 1.3 copy-start.12
  213.4 1.3 copy-start.13
  213.5 91.5 %all-gather.10.cloned.1.call-start = ((), (), s32[]{:S(2)}) async-start(), calls=%async_computation.5 | async-start | bytes 9584640 | tf_op jit(solution)/shard_map/all_gather | solution.py:133
  214.0 176.9 %all-gather.12.cloned.1.call-start = ((), (), s32[]{:S(2)}) async-start(), calls=%async_computation.6 | async-start | bytes 9584640 | tf_op jit(solution)/shard_map/all_gather | solution.py:134
  214.6 204.2 %all-gather.8.cloned.1.call-start = ((), (), s32[]{:S(2)}) async-start(), calls=%async_computation.4 | async-start | bytes 2359296 | tf_op jit(solution)/shard_map/all_gather | solution.py:130
  258.3 208.3 %reduce-scatter.5.cloned.1.call-start = ((), (), s32[]{:S(2)}) async-start(), calls=%async_computation.7 | async-start | bytes 2359296 | tf_op jit(solution)/shard_map/reduce_scatter | solution.py:136
  436.9 0.7 copy-start.8
  436.9 0.7 copy-start.10
  436.9 0.7 copy-start.11
  466.5 1.6 copy-start.4
  466.5 2.0 copy-start.16
  468.6 4.5 copy-start.14
  469.2 3.8 collective-permute-start.7
Sparse Core Ops, SparseCore 0:
  117.2 39.9 all-gather.5
  213.6 41.4 reduce-scatter.2
Sparse Core Ops, SparseCore 1:
  217.0 87.9 all-gather.9
  307.9 82.9 all-gather.11
  392.4 26.4 all-gather.7
  437.0 29.5 reduce-scatter.4
